TPU v7x, 512 devices: a whole 4x8x8 slice. The times are simulated.
512 devices in a mesh: modes: 256 (over y, z, x), grp: 2 (over core).
Axes of the slice: x: 4, y: 8, z: 8, core: 2. Of those that a mesh axis runs over, the one named last changes fastest.
Arguments:
- left_core: bfloat16 [524288, 512], P(('modes', 'grp')), may hold values from -6 to 6
- right_core: bfloat16 [524288, 512], P(('modes', 'grp')), may hold values from -6 to 6
- gauss_core: bfloat16 [524288, 256], P(('modes', 'grp')), may hold values from -0.0078125 to 0.0078125
Outputs:
- left_new: bfloat16 [524288, 256], P(('modes', 'grp'))
- right_new: bfloat16 [524288, 256], P(('modes', 'grp'))
All inputs are finite; a program needn't handle non-finite values.
Results may differ from a plain program's by a relative error of at most 0.0012.
Values sent between devices are 32-bit elements; how exact they have to be, the bound alone decides.
No kernel may reach another device: no remote copies, remote signals or barrier semaphores. Data moves between devices by JAX's collectives and lax.ppermute only.
A program may use at most 64 MiB of HBM per device.

v0:
```python
import math

import jax
import jax.numpy as jnp
from jax import lax
from jax.sharding import Mesh
from jax.sharding import PartitionSpec as P

MODES = ("modes_0", "modes_1", "modes_2")
MODES_GRP = ("modes_0", "modes_1", "modes_2", "grp")


def filled_up(lines, count):
    spare = -lines.shape[0] % count
    if not spare:
        return lines
    return jnp.concatenate([lines, jnp.zeros((spare, *lines.shape[1:]), lines.dtype)])


def from_everyone(x, axis):
    copies = jnp.broadcast_to(x, (lax.axis_size(axis), *x.shape))
    return lax.all_to_all(copies, axis, split_axis=0, concat_axis=0, tiled=True)


def joined_along(tiles, dim):
    tiles = jnp.moveaxis(tiles, 0, dim)
    shape = tiles.shape
    return tiles.reshape(*shape[:dim], shape[dim] * shape[dim + 1], *shape[dim + 2 :])


def whole_of(x, axes, dim):
    far, near = axes
    tiles = from_everyone(from_everyone(x, far), near)
    return joined_along(tiles.swapaxes(0, 1).reshape(-1, *x.shape), dim)


def in_blocks(x, dim, count):
    before, after = (x.shape[:dim], x.shape[dim + 1 :])
    return jnp.moveaxis(x.reshape(*before, count, -1, *after), dim, 0)


def sent_and_summed(x, axis, dim):
    count = lax.axis_size(axis)
    tiles = lax.all_to_all(in_blocks(x, dim, count), axis, 0, 0, tiled=True)
    return jnp.sum(tiles, axis=0)


def summed_rows(x, axes, dim):
    far, near = axes
    tiles = in_blocks(x, dim, lax.axis_size(far))
    nearer = sent_and_summed(tiles, near, dim + 1)
    arrived = lax.all_to_all(nearer, far, split_axis=0, concat_axis=0, tiled=True)
    return arrived.sum(axis=0)


def nested_sum(x, axes):
    padded = filled_up(x, lax.axis_size(axes[0]) * lax.axis_size(axes[1]))
    whole = whole_of(summed_rows(padded, axes, 0), axes, 0)
    return lax.slice_in_dim(whole, 0, len(x)).reshape(x.shape)


def in_one(arrays, axis):
    ends = [0]
    for a in arrays:
        ends.append(ends[-1] + a.size)
    so_far = nested_sum(jnp.concatenate([a.ravel() for a in arrays]), axis)
    return tuple((so_far[b:e].reshape(a.shape) for a, b, e in zip(arrays, ends, ends[1:])))


def contract_rows(first, second, precision=None):
    return lax.dot_general(
        first,
        second,
        (((0,), (0,)), ((), ())),
        precision=precision,
        preferred_element_type=jnp.float32,
    )


def local(left_core, right_core, gauss_core):
    high = lax.Precision.HIGHEST
    local_rows = left_core.shape[0]
    devices = lax.axis_size(MODES) * lax.axis_size("grp")
    norm_scale = math.sqrt(local_rows * devices)
    sketch_part = contract_rows(right_core, gauss_core)
    left_gram = contract_rows(left_core, left_core)
    sketch, left_gram = in_one(
        (sketch_part, left_gram), (("modes_0", "modes_1"), ("modes_2", "grp"))
    )
    tall_sketch = jnp.dot(left_core, sketch, precision=high, preferred_element_type=jnp.float32)
    cross_gram = contract_rows(sketch, left_gram, high)
    gram = jnp.dot(cross_gram, sketch, precision=high)
    chol_lower = jnp.linalg.cholesky(gram)
    q_trans = jax.scipy.linalg.solve_triangular(chol_lower, tall_sketch.T, lower=True)
    projected = jax.scipy.linalg.solve_triangular(chol_lower, cross_gram, lower=True)
    left_new = (q_trans.T * norm_scale).astype(jnp.bfloat16)
    right_new = jnp.dot(
        right_core, (projected / norm_scale).T, precision=high, preferred_element_type=jnp.float32
    ).astype(jnp.bfloat16)
    return (left_new, right_new)


def solution(mesh):
    finer = Mesh(
        mesh.devices.reshape(8, 8, 4, mesh.shape["grp"]), ("modes_0", "modes_1", "modes_2", "grp")
    )
    return jax.shard_map(
        local,
        mesh=finer,
        in_specs=(P(MODES_GRP, None), P(MODES_GRP, None), P(MODES_GRP, None)),
        out_specs=(P(MODES_GRP, None), P(MODES_GRP, None)),
        check_vma=False,
    )
```

profile of v0, /device:TPU:1, one launch (start us, length us, event | category | flops | bytes accessed | tf_op | source)
XLA Modules:
  0.0 195.2 jit_solution(8557719294081953400)
XLA Ops:
  0.6 1.2 copy-done
  1.9 0.7 convolution_bitcast_fusion
  2.6 0.3 copy.24
  2.9 0.9 copy-done.5
  4.0 0.5 convolution_bitcast_fusion.1
  4.4 0.3 copy.23
  4.8 1.5 reshape_reshape.4
  6.3 1.9 copy.16
  8.2 29.8 %all_to_all.28 = f32[8,64,768]{2,1,0:T(8,128)S(1)} all-to-all(f32[8,64,768]{2,1,0:T(8,128)S(1)} %copy.16), channel_id=1, replica_groups=mesh['modes_0'=8,'modes_1'=8,'modes_2'=4,'grp'=2] {'modes_2','grp'}, dimensions={0} | all-to-all | bytes 3145728 | tf_op jit(solution)/shard_map/all_to_all | solution.py:44
  38.1 0.1 all_to_all.19
  38.3 24.3 %all_to_all.29 = f32[64,1,768]{2,1,0:T(1,128)S(1)} all-to-all(f32[64,1,768]{2,1,0:T(1,128)S(1)} %all_to_all.19), channel_id=1, replica_groups=mesh['modes_0'=8,'modes_1'=8,'modes_2'=4,'grp'=2] {'modes_0','modes_1'}, dimensions={0} | all-to-all | bytes 393216 | tf_op jit(solution)/shard_map/all_to_all | solution.py:52
  62.6 0.1 reduce_sum.19
  62.9 16.6 %all_to_all.30 = f32[64,1,768]{2,1,0:T(1,128)S(1)} all-to-all(f32[64,1,768]{2,1,0:T(1,128)S(1)} %broadcast_in_dim.8), channel_id=1, replica_groups=mesh['modes_0'=8,'modes_1'=8,'modes_2'=4,'grp'=2] {'modes_0','modes_1'}, dimensions={0} | all-to-all | bytes 393216 | tf_op jit(solution)/shard_map/all_to_all | solution.py:22
  79.5 1.3 broadcast_in_dim.9
  80.8 6.7 %all-to-all-start.3 = ((f32[8,64,768]{2,1,0:T(8,128)}), f32[8,64,768]{2,1,0:T(8,128)S(1)}, u32[]{:S(2)}, u32[]{:S(2)}) async-start(f32[8,64,768]{2,1,0:T(8,128)} %broadcast_in_dim.9), calls=%async_computation.3 | async-start | bytes 3145728 | tf_op jit(solution)/shard_map/all_to_all | solution.py:22
  87.4 20.6 %all-to-all-done.3 = f32[8,64,768]{2,1,0:T(8,128)S(1)} async-done(((f32[8,64,768]{2,1,0:T(8,128)}), f32[8,64,768]{2,1,0:T(8,128)S(1)}, u32[]{:S(2)}, u32[]{:S(2)}) %all-to-all-start.3) | async-done | bytes 1572896 | tf_op jit(solution)/shard_map/all_to_all | solution.py:22
  108.0 1.2 copy-done.2
  109.2 2.3 %copy.17 = f32[64,8,768]{2,1,0:T(8,128)S(1)} copy(f32[64,8,768]{2,0,1:T(8,128)} %bitcast.57) | data formatting | bytes 3145728 | tf_op jit(solution)/shard_map/transpose | solution.py:34
  111.5 1.5 slice.74
  113.0 1.6 slice.76
  114.6 2.6 %fusion.1 = f32[256,512]{1,0:T(8,128)S(1)} fusion(f32[768,512]{1,0:T(8,128)} %slice.76, f32[1536,256]{1,0:T(8,128)} %slice.74), kind=kOutput, calls=%fused_computation.10 | convolution fusion | flops 805306368 | bytes 2097152 | tf_op jit(solution)/shard_map/dot_general | solution.py:71
  117.2 0.6 fusion.11
  117.8 0.8 copy.19
  118.6 1.0 fusion.16
  119.6 0.7 copy-done.6
  120.3 11.7 %cholesky.50 = f32[128,128]{1,0:T(8,128)S(1)} custom-call(f32[128,128]{1,0:T(8,128)S(1)} %cholesky.118), custom_call_target="Cholesky" | custom-call | tf_op jit(solution)/shard_map/jit(cholesky)/cholesky | solution.py:93
  132.1 2.8 %fusion.9 = f32[256,1024]{1,0:T(8,128)} fusion(bf16[1024,512]{1,0:T(8,128)(2,1)S(1)} %copy-done, f32[1536,256]{1,0:T(8,128)S(1)} %copy-done.1), kind=kOutput, calls=%fused_computation.20 | convolution fusion | flops 1610612736 | bytes 2621440 | tf_op jit(solution)/shard_map/dot_general | solution.py:90
  134.9 9.8 %custom-call.18 = f32[1,128,128]{1,2,0:T(8,128)S(1)} custom-call(f32[1,128,128]{2,1,0:T(8,128)S(1)} %get-tuple-element.31), custom_call_target="InvertDiagBlocksLowerTriangular" | custom-call | tf_op jit(solution)/shard_map/jit(cholesky)/cholesky | solution.py:93
  144.7 1.0 constant_dynamic-update-slice_fusion.1
  145.8 1.1 convolution_subtract_fusion.2
  146.9 11.9 %cholesky.105 = f32[128,128]{1,0:T(8,128)S(1)} custom-call(f32[128,128]{1,0:T(8,128)S(1)} %convolution_subtract_fusion.2), custom_call_target="Cholesky" | custom-call | tf_op jit(solution)/shard_map/jit(cholesky)/cholesky | solution.py:93
  158.8 0.7 compare_reduce_fusion
  160.8 1.0 select_select_fusion
  161.9 5.3 %while.1 = (s32[]{:T(128)}, f32[256,256]{1,0:T(8,128)S(1)}, s32[2,2]{1,0:T(2,128)S(1)}, f32[2,128,128]{2,1,0:T(8,128)}, s32[]{:T(128)}) while((s32[]{:T(128)}, f32[256,256]{1,0:T(8,128)S(1)}, s32[2,2]{1,0:T(2,128)S(1)}, f32[2,128,128]{2,1,0:T(8,128)}, s32[]{:T(128)}) %tuple.31), condition=%wide.while_cond, body=%wide.while_body.sunk | while | flops 2 | bytes 132705 | solution.py:94
  161.9 0.6 fusion.42
  162.5 2.1 %bitcast_dynamic-update-slice_fusion.2 = f32[2,128,128]{2,1,0:T(8,128)} fusion(f32[2,128,128]{2,1,0:T(8,128)} %get-tuple-element.73, s32[]{:T(128)} %get-tuple-element.70, f32[256,256]{1,0:T(8,128)S(1)} %get-tuple-element.76, s32[]{:T(128)} %bitcast.55, s32[]{:T(128)} %bitcast.56), kind=kLoop, calls=%fused_computation.clone.1 | loop fusion | bytes 132608 | tf_op jit(solution)/shard_map/jit(_solve_triangular)/triangular_solve
  164.5 0.6 fusion.42
  165.1 2.1 %bitcast_dynamic-update-slice_fusion.2 = f32[2,128,128]{2,1,0:T(8,128)} fusion(f32[2,128,128]{2,1,0:T(8,128)} %get-tuple-element.73, s32[]{:T(128)} %get-tuple-element.70, f32[256,256]{1,0:T(8,128)S(1)} %get-tuple-element.76, s32[]{:T(128)} %bitcast.55, s32[]{:T(128)} %bitcast.56), kind=kLoop, calls=%fused_computation.clone.1 | loop fusion | bytes 132608 | tf_op jit(solution)/shard_map/jit(_solve_triangular)/triangular_solve
  167.2 20.5 %custom-call.19 = f32[2,128,128]{1,2,0:T(8,128)S(1)} custom-call(f32[2,128,128]{2,1,0:T(8,128)} %get-tuple-element.9), custom_call_target="InvertDiagBlocksLowerTriangular" | custom-call | tf_op jit(solution)/shard_map/jit(_solve_triangular)/triangular_solve | solution.py:94
  187.7 0.4 fusion.14
  188.1 0.4 convolution_subtract_fusion.1
  188.5 0.4 fusion.21
  188.9 2.3 %fusion = bf16[1024,256]{0,1:T(8,128)(2,1)S(1)} fusion(bf16[1024,512]{1,0:T(8,128)(2,1)} %param.4, f32[128,512]{1,0:T(8,128)S(1)} %fusion.21, f32[128,512]{1,0:T(8,128)S(1)} %fusion.14), kind=kOutput, calls=%fused_computation.5 | convolution fusion | flops 1611137024 | bytes 2097152 | tf_op jit(solution)/shard_map/dot_general | solution.py:97
  191.3 1.0 copy.21
  192.3 0.6 fusion.5
  192.9 0.6 convolution_subtract_fusion
  193.5 0.6 fusion.22
  194.2 1.0 copy.20
  (26 shorter events, 0.7 us)
Async XLA Ops:
  0.6 1.2 copy-start
  2.6 1.2 copy-start.5
  2.6 1.3 copy-start.7
  80.8 27.3 %all-to-all-start.3 = ((f32[8,64,768]{2,1,0:T(8,128)}), f32[8,64,768]{2,1,0:T(8,128)S(1)}, u32[]{:S(2)}, u32[]{:S(2)}) async-start(f32[8,64,768]{2,1,0:T(8,128)} %broadcast_in_dim.9), calls=%async_computation.3 | async-start | bytes 3145728 | tf_op jit(solution)/shard_map/all_to_all | solution.py:22
  108.0 1.2 copy-start.2
  114.6 2.6 %copy-start.1 = (f32[1536,256]{1,0:T(8,128)S(1)}, f32[1536,256]{1,0:T(8,128)}, u32[]{:S(2)}) copy-start(f32[1536,256]{1,0:T(8,128)} %slice.74) | copy-start | bytes 4718596
  119.6 0.7 copy-start.6
  158.8 2.0 %copy-start.4 = (f32[256,256]{1,0:T(8,128)}, f32[256,256]{1,0:T(8,128)S(1)}, u32[]{:S(2)}) copy-start(f32[256,256]{1,0:T(8,128)S(1)} %get-tuple-element.29) | copy-start | bytes 786436
  188.9 3.4 %copy-start.3 = (f32[256,1024]{1,0:T(8,128)S(1)}, f32[256,1024]{1,0:T(8,128)}, u32[]{:S(2)}) copy-start(f32[256,1024]{1,0:T(8,128)} %fusion.9) | copy-start | bytes 3145732
where the time goes:
time: 196 us; the launch traced here: 195 us
  blocking collectives  70.8 us (36%)
  other arithmetic  57.1 us (29%)
  local copies, waits for them, and re-layouts  23.3 us (12%)
  waiting for transfers between devices  20.6 us (11%)
  matrix products  14.7 us (8%)
  starting transfers between devices  6.65 us (3%)
  between operations  2.13 us (1%)
    another operation x6, other arithmetic, local(): chol_lower = jnp.linalg.cholesky(gram)  34.2 us
    all_to_all x1, blocking collectives, sent_and_summed(): tiles = lax.all_to_all(in_blocks(x, dim, count), axis, 0, 0, tiled=True)  29.8 us
    all_to_all x1, blocking collectives, summed_rows(): lax.all_to_all(nearer, far, split_axis=0, concat_axis=0, tiled=True)  24.3 us
    another operation x3, other arithmetic, local(): jax.scipy.linalg.solve_triangular(chol_lower, tall_sketch.T, lower=True)  21.5 us
    all_to_all x1, waiting for transfers between devices, from_everyone(): return lax.all_to_all(copies, axis, split_axis=0, concat_axis=0, tiled=True)  20.6 us
    all_to_all x1, blocking collectives, from_everyone(): return lax.all_to_all(copies, axis, split_axis=0, concat_axis=0, tiled=True)  16.6 us
    unnamed x21, local copies, waits for them, and re-layouts  6.71 us
    all_to_all x1, starting transfers between devices, from_everyone(): return lax.all_to_all(copies, axis, split_axis=0, concat_axis=0, tiled=True)  6.65 us
  transfers between devices with their start and end apart: 1, of which 1 were waited for; matrix products, arithmetic and copies ran while one was open for 0% of the time, Pallas kernels for 0%

commit v1 on v0

v1 whole, which is shorter than its diff:
```python
import math

import jax
import jax.numpy as jnp
from jax import lax
from jax.experimental import pallas as pl
from jax.experimental.pallas import tpu as pltpu
from jax.sharding import Mesh
from jax.sharding import PartitionSpec as P

GRID = ("modes_0", "modes_1", "modes_2", "grp")
PLANE = ("modes_1", "modes_2")
HI = lax.Precision.HIGHEST
F32, BF16 = jnp.float32, jnp.bfloat16
T = 128
SUB = 8
ANY = pl.BlockSpec(memory_space=pl.ANY)
VMEM = pl.BlockSpec(memory_space=pltpu.VMEM)
SMEM = pl.BlockSpec(memory_space=pltpu.SMEM)


def dot(x, y, dims=((1,), (0,)), precision=HI):
    return lax.dot_general(x, y, (dims, ((), ())), precision=precision, preferred_element_type=F32)


def tiles_of(rank, target):
    sketch = [("s", i, j) for j in range(target // T) for i in range(rank // T)]
    gram = [("g", i, j) for j in range(rank // T) for i in range(j, rank // T)]
    both = sketch + gram
    return both[: len(both) // 2], both[len(both) // 2 :]


def local_products(core_ref, left_hbm, right_hbm, gauss_hbm, keep_ref, send_ref, left, right, gauss, sems):
    copies = [
        pltpu.make_async_copy(src, dst, sems.at[i])
        for i, (src, dst) in enumerate(((right_hbm, right), (gauss_hbm, gauss), (left_hbm, left)))
    ]
    for copy in copies:
        copy.start()
    rank, target = right.shape[1], gauss.shape[1]
    halves = tiles_of(rank, target)
    core = core_ref[0]

    def put(kind, col, value, first):
        for i in range(value.shape[0] // T):
            tile = (kind, first + i, col)
            half = 0 if tile in halves[0] else 1
            place = halves[half].index(tile)
            block = value[i * T : (i + 1) * T, :]

            @pl.when(core == half)
            def _():
                keep_ref[place] = block

            @pl.when(core != half)
            def _():
                send_ref[place] = block

    copies[0].wait()
    copies[1].wait()
    x = dot(right[...], gauss[...], ((0,), (0,)), None)
    for j in range(target // T):
        put("s", j, x[:, j * T : (j + 1) * T], 0)
    copies[2].wait()
    for j in range(0, rank // T, 2):
        y = dot(left[:, j * T :], left[:, j * T : (j + 2) * T], ((0,), (0,)), None)
        put("g", j, y[:, :T], j)
        put("g", j + 1, y[T:, T:], j + 1)


def products(core, left_core, right_core, gauss_core):
    rank, target = right_core.shape[1], gauss_core.shape[1]
    half = jax.ShapeDtypeStruct((len(tiles_of(rank, target)[0]), T, T), F32)
    return pl.pallas_call(
        local_products,
        out_shape=(half, half),
        in_specs=[SMEM, ANY, ANY, ANY],
        out_specs=[VMEM, VMEM],
        scratch_shapes=[
            pltpu.VMEM(left_core.shape, BF16),
            pltpu.VMEM(right_core.shape, BF16),
            pltpu.VMEM(gauss_core.shape, BF16),
            pltpu.SemaphoreType.DMA((3,)),
        ],
        name="products",
    )(core, left_core, right_core, gauss_core)


def lane_of(x, c):
    return jnp.take_along_axis(x, jnp.full(x.shape, c, jnp.int32), axis=1)


def row_of(x, k):
    return lax.broadcast_in_dim(x[k : k + 1, :], x.shape, (0, 1))


def inverse_factor_of_tile(a):
    lane = lax.broadcasted_iota(jnp.int32, (SUB, T), 1)
    sub = lax.broadcasted_iota(jnp.int32, (SUB, T), 0)
    rows = [a[SUB * i : SUB * (i + 1), :] for i in range(T // SUB)]
    out = []
    for s in range(T // SUB):
        base = SUB * s
        own = (lane >= base) & (lane < base + SUB)
        w = rows[s]
        cols = [lane_of(w, base + k) for k in range(SUB)]
        w = jnp.where(own, jnp.where(lane == sub + base, 1.0, 0.0), w)
        f = jnp.zeros((SUB, T), F32)
        for k in range(SUB):
            here = sub == k
            pivot = row_of(cols[k], k)
            inverse = 1.0 / pivot
            row = row_of(w, k)
            f = jnp.where(here, row * lax.rsqrt(pivot), f)
            for j in range(k + 1, SUB):
                t = row_of(cols[j], k) * inverse
                cols[j] = jnp.where(here, t, cols[j] - cols[k] * t)
            t = row * inverse
            w = jnp.where(here, t, w - cols[k] * t)
        out.append(jnp.where(lane <= sub + base, f, 0.0))
        ws = [row_of(w, k) for k in range(SUB)]
        for i in range(s + 1, T // SUB):
            r = rows[i]
            m = [lane_of(r, base + k) for k in range(SUB)]
            r = jnp.where(own, 0.0, r)
            for k in range(SUB):
                r = r - m[k] * ws[k]
            rows[i] = r
    return jnp.concatenate(out, 0)


def split(x):
    high = x.astype(BF16)
    return high, (x - high.astype(F32)).astype(BF16)


def truncate(norm, core_ref, mine_ref, theirs_ref, left_hbm, right_hbm, left_new_ref, right_new_ref,
             left, right, tiles, sketch, gram_left, sems):
    copies = [
        pltpu.make_async_copy(left_hbm, left, sems.at[0]),
        pltpu.make_async_copy(right_hbm, right, sems.at[1]),
    ]
    for copy in copies:
        copy.start()
    core = core_ref[0]
    tiles[core] = mine_ref[...]
    tiles[1 - core] = theirs_ref[...]
    rank, target = sketch.shape
    for half, held in enumerate(tiles_of(rank, target)):
        for place, (kind, i, j) in enumerate(held):
            tile = tiles[half, place]
            if kind == "s":
                sketch[i * T : (i + 1) * T, j * T : (j + 1) * T] = tile
            else:
                gram_left[i * T : (i + 1) * T, j * T : (j + 1) * T] = tile
                if i != j:
                    gram_left[j * T : (j + 1) * T, i * T : (i + 1) * T] = tile.T
    s = sketch[...]
    cross = dot(gram_left[...], s)
    gram = dot(s, cross, ((0,), (0,)))
    m11 = inverse_factor_of_tile(gram[:T, :T])
    u12 = dot(m11, gram[:T, T:])
    m22 = inverse_factor_of_tile(gram[T:, T:] - dot(u12, u12, ((0,), (0,))))
    m21 = -dot(m22, dot(u12, m11, ((0,), (0,))))
    m = jnp.concatenate(
        [jnp.concatenate([m11, jnp.zeros_like(m11)], 1), jnp.concatenate([m21, m22], 1)], 0
    )
    for scale, factor, copy, held, out_ref in (
        (norm, s, copies[0], left, left_new_ref),
        (1.0 / norm, cross, copies[1], right, right_new_ref),
    ):
        high, low = split(dot(factor, m, ((1,), (1,))) * scale)
        copy.wait()
        x = held[...]
        out_ref[...] = (dot(x, high, precision=None) + dot(x, low, precision=None)).astype(BF16)


def truncated(norm, core, mine, theirs, left_core, right_core, target):
    rows, rank = left_core.shape
    import functools
    out = jax.ShapeDtypeStruct((rows, target), BF16)
    return pl.pallas_call(
        functools.partial(truncate, norm),
        out_shape=(out, out),
        in_specs=[SMEM, VMEM, VMEM, ANY, ANY],
        out_specs=[VMEM, VMEM],
        scratch_shapes=[
            pltpu.VMEM(left_core.shape, BF16),
            pltpu.VMEM(right_core.shape, BF16),
            pltpu.VMEM((2, *mine.shape), F32),
            pltpu.VMEM((rank, target), F32),
            pltpu.VMEM((rank, rank), F32),
            pltpu.SemaphoreType.DMA((2,)),
        ],
        name="truncate",
    )(core, mine, theirs, left_core, right_core)


def to_all(x, axes, count):
    return lax.all_to_all(jnp.broadcast_to(x, (count, *x.shape)), axes, 0, 0, tiled=True)


def local(left_core, right_core, gauss_core):
    devices = math.prod(lax.axis_size(a) for a in GRID)
    plane = lax.axis_size(PLANE[0]) * lax.axis_size(PLANE[1])
    norm = math.sqrt(left_core.shape[0] * devices)
    core = lax.axis_index("grp").reshape(1)
    swap = [(0, 1), (1, 0)]
    keep, send = products(core, left_core, right_core, gauss_core)
    x = keep + lax.ppermute(send, "grp", swap)
    x = lax.all_to_all(x.reshape(plane, -1, 4, T), PLANE, 0, 0, tiled=True).sum(0)
    x = to_all(x, "modes_0", lax.axis_size("modes_0")).reshape(-1, *x.shape).sum(0)
    mine = to_all(x, PLANE, plane).reshape(keep.shape)
    theirs = lax.ppermute(mine, "grp", swap)
    return truncated(norm, core, mine, theirs, left_core, right_core, gauss_core.shape[1])


def solution(mesh):
    finer = Mesh(mesh.devices.reshape(8, 8, 4, mesh.shape["grp"]), GRID)
    spec = P(GRID, None)
    return jax.shard_map(
        local, mesh=finer, in_specs=(spec, spec, spec), out_specs=(spec, spec), check_vma=False
    )
```

time: 196 us -> 104 us (0.53)
  other arithmetic: 57.1 us -> 1.27 us
  local copies, waits for them, and re-layouts: 23.3 us -> 0.91 us
  Pallas kernels: 0 us -> 21.9 us
  waiting for transfers between devices: 20.6 us -> 3.25 us
  matrix products: 14.7 us -> 0 us
  blocking collectives: 70.8 us -> 59.6 us
  starting transfers between devices: 6.65 us -> 16.3 us
    another operation x9 -> x0, other arithmetic: 55.7 us -> none  [the longest x6 34.2 us: local(): chol_lower = jnp.linalg.cholesky(gram)]
    pallas_call x0 -> x2, Pallas kernels: none -> 21.9 us  [the longest x1 17.6 us: truncated(): pl.pallas_call(functools.partial(truncate, norm), out_shape=(out, out), i...]
    all_to_all x1 -> x0, waiting for transfers between devices: 20.6 us -> none  [from_everyone(): return lax.all_to_all(copies, axis, split_axis=0, concat_axis=0, tiled=True)]
    ppermute x0 -> x2, starting transfers between devices: none -> 16.3 us  [the longest x1 8.75 us: local(): x = keep + lax.ppermute(send, 'grp', swap)]
    all_to_all x3, blocking collectives: 70.8 us -> 59.6 us  [the longest x2 34.6 us: to_all(): lax.all_to_all(jnp.broadcast_to(x, (count, *x.shape)), axes, 0, 0, tiled=...]
    dot_general x6 -> x0, matrix products: 9.53 us -> none  [the longest x3 3.76 us: contract_rows(): lax.dot_general(first, second, (((0,), (0,)), ((), ())), precision=precis...]
    another operation x10 -> x0, local copies, waits for them, and re-layouts: 6.87 us -> none
    all_to_all x1 -> x0, starting transfers between devices: 6.65 us -> none  [from_everyone(): return lax.all_to_all(copies, axis, split_axis=0, concat_axis=0, tiled=True)]
  transfers between devices with their start and end apart: 1 -> 2, of which waited for: 1 -> 2; matrix products, arithmetic and copies ran while one was open for 0% -> 0% of each run, Pallas kernels for 0% -> 0%
where the time goes in v1:
time: 104 us
  blocking collectives  59.6 us (57%)
  Pallas kernels  21.9 us (21%)
  starting transfers between devices  16.3 us (16%)
  waiting for transfers between devices  3.25 us (3%)
  other arithmetic  1.27 us (1%)
    all_to_all x2, blocking collectives, to_all(): lax.all_to_all(jnp.broadcast_to(x, (count, *x.shape)), axes, 0, 0, tiled=...  34.6 us
    all_to_all x1, blocking collectives, local(): lax.all_to_all(x.reshape(plane, -1, 4, T), PLANE, 0, 0, tiled=True).sum(0)  25 us
    pallas_call x1, Pallas kernels, truncated(): pl.pallas_call(functools.partial(truncate, norm), out_shape=(out, out), i...  17.6 us
    ppermute x1, starting transfers between devices, local(): x = keep + lax.ppermute(send, 'grp', swap)  8.75 us
    ppermute x1, starting transfers between devices, local(): theirs = lax.ppermute(mine, 'grp', swap)  7.56 us
    pallas_call x1, Pallas kernels, products(): pl.pallas_call(local_products, out_shape=(half, half), in_specs=[SMEM, AN...  4.24 us
  transfers between devices with their start and end apart: 2, of which 2 were waited for; matrix products, arithmetic and copies ran while one was open for 0% of the time, Pallas kernels for 0%

profile of v1, /device:TPU:1, one launch (start us, length us, event | category | flops | bytes accessed | tf_op | source)
XLA Modules:
  0.0 104.0 jit_solution(10118847573426067853)
XLA Ops:
  0.6 4.2 %products.1 = (f32[9,128,128]{2,1,0:T(8,128)}, f32[9,128,128]{2,1,0:T(8,128)}) custom-call(s32[1]{0:T(128)} %bitcast.core_ref, bf16[1024,512]{1,0:T(8,128)(2,1)} %left_hbm.3, bf16[1024,512]{1,0:T(8,128)(2,1)} %right_hbm.3, bf16[1024,256]{1,0:T(8,128)(2,1)} %gauss_hbm.1), custom_call_target="tpu_custom_call" | custom-call | tf_op jit(solution)/shard_map/products/pallas_call | solution.py:74
  4.9 8.7 %collective-permute-start = (f32[9,128,128]{2,1,0:T(8,128)}, f32[9,128,128]{2,1,0:T(8,128)S(1)}, u32[]{:S(2)}, u32[]{:S(2)}) collective-permute-start(f32[9,128,128]{2,1,0:T(8,128)} %get-tuple-element.5), channel_id=1, source_target_pairs={{0,1},{1,0},{2,3},{3,2},{4,5},{5,4},{6,7},{7,6},{8,9},{9,8},{10,11... | collective-permute-start | bytes 1769480 | tf_op jit(solution)/shard_map/ppermute | solution.py:210
  13.6 1.8 %collective-permute-done = f32[9,128,128]{2,1,0:T(8,128)S(1)} collective-permute-done((f32[9,128,128]{2,1,0:T(8,128)}, f32[9,128,128]{2,1,0:T(8,128)S(1)}, u32[]{:S(2)}, u32[]{:S(2)}) %collective-permute-start) | collective-permute-done | bytes 589856 | tf_op jit(solution)/shard_map/ppermute | solution.py:210
  15.5 1.1 %add.3 = f32[9,128,128]{2,1,0:T(8,128)S(1)} add(f32[9,128,128]{2,1,0:T(8,128)} %get-tuple-element.4, f32[9,128,128]{2,1,0:T(8,128)S(1)} %collective-permute-done) | non-fusion elementwise | flops 147456 | bytes 1769472 | tf_op jit(solution)/shard_map/add | solution.py:210
  16.6 25.0 %all_to_all.15 = f32[32,9,4,128]{3,2,1,0:T(4,128)S(1)} all-to-all(f32[32,9,4,128]{3,2,1,0:T(4,128)S(1)} %bitcast.3), channel_id=1, replica_groups=mesh['modes_0'=8,'modes_1'=8,'modes_2'=4,'grp'=2] {'modes_1','modes_2'}, dimensions={0} | all-to-all | bytes 1179648 | tf_op jit(solution)/shard_map/all_to_all | solution.py:211
  41.6 0.1 reduce_sum.18
  41.7 14.8 %all_to_all.16 = f32[8,9,4,128]{3,2,1,0:T(4,128)S(1)} all-to-all(f32[8,9,4,128]{3,2,1,0:T(4,128)S(1)} %broadcast_in_dim.6), channel_id=1, replica_groups=mesh['modes_0'=8,'modes_1'=8,'modes_2'=4,'grp'=2] {'modes_0'}, dimensions={0} | all-to-all | bytes 294912 | tf_op jit(solution)/shard_map/all_to_all | solution.py:200
  56.6 0.1 broadcast_in_dim.7
  56.6 19.8 %all_to_all.17 = f32[32,9,4,128]{3,2,1,0:T(4,128)S(1)} all-to-all(f32[32,9,4,128]{3,2,1,0:T(4,128)S(1)} %broadcast_in_dim.7), channel_id=1, replica_groups=mesh['modes_0'=8,'modes_1'=8,'modes_2'=4,'grp'=2] {'modes_1','modes_2'}, dimensions={0} | all-to-all | bytes 1179648 | tf_op jit(solution)/shard_map/all_to_all | solution.py:200
  76.4 0.0 copy-start
  76.4 7.6 %collective-permute-start.1 = (f32[9,128,128]{2,1,0:T(8,128)S(1)}, f32[9,128,128]{2,1,0:T(8,128)S(1)}, u32[]{:S(2)}, u32[]{:S(2)}) collective-permute-start(f32[9,128,128]{2,1,0:T(8,128)S(1)} %bitcast.4), channel_id=1, source_target_pairs={{0,1},{1,0},{2,3},{3,2},{4,5},{5,4},{6,7},{7,6},{8,9},{9,8},{10,11... | collective-permute-start | bytes 1769480 | tf_op jit(solution)/shard_map/ppermute | solution.py:214
  84.0 1.4 %collective-permute-done.1.theirs_ref = f32[9,128,128]{2,1,0:T(8,128)S(1)} collective-permute-done((f32[9,128,128]{2,1,0:T(8,128)S(1)}, f32[9,128,128]{2,1,0:T(8,128)S(1)}, u32[]{:S(2)}, u32[]{:S(2)}) %collective-permute-start.1) | collective-permute-done | bytes 589856 | tf_op jit(solution)/shard_map/ppermute | solution.py:214
  85.4 0.0 copy-done
  85.4 0.0 copy-start.1
  85.4 0.8 copy-done.1
  86.2 17.6 %truncate.1 = (bf16[1024,256]{1,0:T(8,128)(2,1)}, bf16[1024,256]{1,0:T(8,128)(2,1)}) custom-call(s32[1]{0:T(128)} %bitcast.core_ref, f32[9,128,128]{2,1,0:T(8,128)} %bitcast.5, f32[9,128,128]{2,1,0:T(8,128)} %copy-done.1, bf16[1024,512]{1,0:T(8,128)(2,1)} %left_hbm.3, bf16[1024,512]{1,0:T(8,128)(2,1)} %right_hbm.3), custom_call_target="tpu_custom_call" | custom-call | tf_op jit(solution)/shard_map/truncate/pallas_call | solution.py:182
  (2 shorter events, 0.1 us)
Async XLA Ops:
  4.9 10.6 %collective-permute-start = (f32[9,128,128]{2,1,0:T(8,128)}, f32[9,128,128]{2,1,0:T(8,128)S(1)}, u32[]{:S(2)}, u32[]{:S(2)}) collective-permute-start(f32[9,128,128]{2,1,0:T(8,128)} %get-tuple-element.5), channel_id=1, source_target_pairs={{0,1},{1,0},{2,3},{3,2},{4,5},{5,4},{6,7},{7,6},{8,9},{9,8},{10,11... | collective-permute-start | bytes 1769480 | tf_op jit(solution)/shard_map/ppermute | solution.py:210
  76.4 9.0 %copy-start = (f32[32,9,4,128]{3,2,1,0:T(4,128)}, f32[32,9,4,128]{3,2,1,0:T(4,128)S(1)}, u32[]{:S(2)}) copy-start(f32[32,9,4,128]{3,2,1,0:T(4,128)S(1)} %all_to_all.17) | copy-start | bytes 1769476
  76.4 9.0 %collective-permute-start.1 = (f32[9,128,128]{2,1,0:T(8,128)S(1)}, f32[9,128,128]{2,1,0:T(8,128)S(1)}, u32[]{:S(2)}, u32[]{:S(2)}) collective-permute-start(f32[9,128,128]{2,1,0:T(8,128)S(1)} %bitcast.4), channel_id=1, source_target_pairs={{0,1},{1,0},{2,3},{3,2},{4,5},{5,4},{6,7},{7,6},{8,9},{9,8},{10,11... | collective-permute-start | bytes 1769480 | tf_op jit(solution)/shard_map/ppermute | solution.py:214
  85.4 0.8 copy-start.1

commit v2 on v1

--- a/solution.py
+++ b/solution.py
@@ -1,3 +1,4 @@
+import functools
 import math
 
 import jax
@@ -14,6 +15,7 @@
 F32, BF16 = jnp.float32, jnp.bfloat16
 T = 128
 SUB = 8
+OUTER = 32
 ANY = pl.BlockSpec(memory_space=pl.ANY)
 VMEM = pl.BlockSpec(memory_space=pltpu.VMEM)
 SMEM = pl.BlockSpec(memory_space=pltpu.SMEM)
@@ -70,7 +72,7 @@
 
 def products(core, left_core, right_core, gauss_core):
     rank, target = right_core.shape[1], gauss_core.shape[1]
-    half = jax.ShapeDtypeStruct((len(tiles_of(rank, target)[0]), T, T), F32)
+    half = pltpu.VMEM((len(tiles_of(rank, target)[0]), T, T), F32)
     return pl.pallas_call(
         local_products,
         out_shape=(half, half),
@@ -87,46 +89,19 @@
 
 
 def lane_of(x, c):
-    return jnp.take_along_axis(x, jnp.full(x.shape, c, jnp.int32), axis=1)
+    x = x[c // T]
+    return jnp.take_along_axis(x, jnp.full(x.shape, c % T, jnp.int32), axis=1)
 
 
 def row_of(x, k):
     return lax.broadcast_in_dim(x[k : k + 1, :], x.shape, (0, 1))
 
 
-def inverse_factor_of_tile(a):
-    lane = lax.broadcasted_iota(jnp.int32, (SUB, T), 1)
-    sub = lax.broadcasted_iota(jnp.int32, (SUB, T), 0)
-    rows = [a[SUB * i : SUB * (i + 1), :] for i in range(T // SUB)]
-    out = []
-    for s in range(T // SUB):
-        base = SUB * s
-        own = (lane >= base) & (lane < base + SUB)
-        w = rows[s]
-        cols = [lane_of(w, base + k) for k in range(SUB)]
-        w = jnp.where(own, jnp.where(lane == sub + base, 1.0, 0.0), w)
-        f = jnp.zeros((SUB, T), F32)
-        for k in range(SUB):
-            here = sub == k
-            pivot = row_of(cols[k], k)
-            inverse = 1.0 / pivot
-            row = row_of(w, k)
-            f = jnp.where(here, row * lax.rsqrt(pivot), f)
-            for j in range(k + 1, SUB):
-                t = row_of(cols[j], k) * inverse
-                cols[j] = jnp.where(here, t, cols[j] - cols[k] * t)
-            t = row * inverse
-            w = jnp.where(here, t, w - cols[k] * t)
-        out.append(jnp.where(lane <= sub + base, f, 0.0))
-        ws = [row_of(w, k) for k in range(SUB)]
-        for i in range(s + 1, T // SUB):
-            r = rows[i]
-            m = [lane_of(r, base + k) for k in range(SUB)]
-            r = jnp.where(own, 0.0, r)
-            for k in range(SUB):
-                r = r - m[k] * ws[k]
-            rows[i] = r
-    return jnp.concatenate(out, 0)
+def tree_sum(terms):
+    while len(terms) > 1:
+        rest = terms[len(terms) // 2 * 2 :]
+        terms = [x + y for x, y in zip(terms[::2], terms[1::2])] + rest
+    return terms[0]
 
 
 def split(x):
@@ -134,64 +109,140 @@
     return high, (x - high.astype(F32)).astype(BF16)
 
 
+def dot_split(x, y, dims=((1,), (0,))):
+    (xh, xl), (yh, yl) = x, y
+    return dot(xh, yh, dims, None) + (dot(xh, yl, dims, None) + dot(xl, yh, dims, None))
+
+
+def inverse_factor(a):
+    n = a.shape[0]
+    parts = range(n // T)
+    sub = lax.broadcasted_iota(jnp.int32, (SUB, T), 0)
+    lanes = [lax.broadcasted_iota(jnp.int32, (SUB, T), 1) + T * h for h in parts]
+    done = []
+    for first in range(0, n, OUTER):
+        block = a[first : first + OUTER, :]
+        if first:
+            u = jnp.concatenate(done, 0)
+            row = lax.broadcasted_iota(jnp.int32, u.shape, 0)
+            col = lax.broadcasted_iota(jnp.int32, u.shape, 1)
+            x = dot_split(
+                split(u[:, first : first + OUTER]),
+                split(jnp.where((col <= row) | (col >= first), u, 0.0)),
+                ((0,), (0,)),
+            )
+            col = lax.broadcasted_iota(jnp.int32, block.shape, 1)
+            block = jnp.where(col >= first, block, 0.0) - x
+        rows = [
+            [block[i : i + SUB, T * h : T * (h + 1)] for h in parts] for i in range(0, OUTER, SUB)
+        ]
+        for s in range(OUTER // SUB):
+            base = first + SUB * s
+            here_part = base // T
+            lane = lanes[here_part]
+            own = (lane >= base) & (lane < base + SUB)
+            w = list(rows[s])
+            cols = [lane_of(w, base + k) for k in range(SUB)]
+            w[here_part] = jnp.where(
+                own, jnp.where(lane == sub + base, 1.0, 0.0), w[here_part]
+            )
+            f = [jnp.zeros((SUB, T), F32)] * len(w)
+            pivot = row_of(cols[0], 0)
+            for k in range(SUB):
+                here = sub == k
+                inverse, root = 1.0 / pivot, lax.rsqrt(pivot)
+                for j in range(k + 1, SUB):
+                    r = row_of(cols[j], k)
+                    if j == k + 1:
+                        rest = cols[j] - (cols[k] * r) * inverse
+                        pivot = row_of(rest, j)
+                        cols[j] = jnp.where(here, r * inverse, rest)
+                    else:
+                        t = r * inverse
+                        cols[j] = jnp.where(here, t, cols[j] - cols[k] * t)
+                for h in parts:
+                    r = row_of(w[h], k)
+                    f[h] = jnp.where(here, r * root, f[h])
+                    t = r * inverse
+                    w[h] = jnp.where(here, t, w[h] - cols[k] * t)
+            keep = [(lanes[h] <= sub + base) | (lanes[h] >= first + OUTER) for h in parts]
+            done.append(jnp.concatenate([jnp.where(keep[h], f[h], 0.0) for h in parts], 1))
+            ws = [[row_of(w[h], k) for k in range(SUB)] for h in parts]
+            for i in range(s + 1, OUTER // SUB):
+                m = [lane_of(rows[i], base + k) for k in range(SUB)]
+                r = list(rows[i])
+                r[here_part] = jnp.where(own, 0.0, r[here_part])
+                rows[i] = [r[h] - tree_sum([x * y for x, y in zip(m, ws[h])]) for h in parts]
+    m = jnp.concatenate(done, 0)
+    row = lax.broadcasted_iota(jnp.int32, m.shape, 0)
+    col = lax.broadcasted_iota(jnp.int32, m.shape, 1)
+    return jnp.where(row >= col, m, 0.0)
+
+
 def truncate(norm, core_ref, mine_ref, theirs_ref, left_hbm, right_hbm, left_new_ref, right_new_ref,
-             left, right, tiles, sketch, gram_left, sems):
+             left, right, sketch, gram_left, tile_sems, sems):
+    rank, target = sketch.shape
+    halves = tiles_of(rank, target)
+    core = core_ref[0]
+
+    def place(half, i):
+        kind, row, col = halves[half][i]
+        ref = sketch if kind == "s" else gram_left
+        return ref.at[pl.ds(row * T, T), pl.ds(col * T, T)]
+
+    for own in range(2):
+
+        @pl.when(core == own)
+        def _():
+            for half in range(2):
+                src = mine_ref if half == own else theirs_ref
+                for i in range(len(halves[half])):
+                    pltpu.make_async_copy(src.at[i], place(half, i), tile_sems.at[half, i]).start()
+
     copies = [
         pltpu.make_async_copy(left_hbm, left, sems.at[0]),
         pltpu.make_async_copy(right_hbm, right, sems.at[1]),
     ]
     for copy in copies:
         copy.start()
-    core = core_ref[0]
-    tiles[core] = mine_ref[...]
-    tiles[1 - core] = theirs_ref[...]
-    rank, target = sketch.shape
-    for half, held in enumerate(tiles_of(rank, target)):
-        for place, (kind, i, j) in enumerate(held):
-            tile = tiles[half, place]
-            if kind == "s":
-                sketch[i * T : (i + 1) * T, j * T : (j + 1) * T] = tile
-            else:
-                gram_left[i * T : (i + 1) * T, j * T : (j + 1) * T] = tile
-                if i != j:
-                    gram_left[j * T : (j + 1) * T, i * T : (i + 1) * T] = tile.T
-    s = sketch[...]
-    cross = dot(gram_left[...], s)
-    gram = dot(s, cross, ((0,), (0,)))
-    m11 = inverse_factor_of_tile(gram[:T, :T])
-    u12 = dot(m11, gram[:T, T:])
-    m22 = inverse_factor_of_tile(gram[T:, T:] - dot(u12, u12, ((0,), (0,))))
-    m21 = -dot(m22, dot(u12, m11, ((0,), (0,))))
-    m = jnp.concatenate(
-        [jnp.concatenate([m11, jnp.zeros_like(m11)], 1), jnp.concatenate([m21, m22], 1)], 0
-    )
-    for scale, factor, copy, held, out_ref in (
-        (norm, s, copies[0], left, left_new_ref),
-        (1.0 / norm, cross, copies[1], right, right_new_ref),
-    ):
-        high, low = split(dot(factor, m, ((1,), (1,))) * scale)
+    for half in range(2):
+        for i in range(len(halves[half])):
+            pltpu.make_async_copy(mine_ref.at[i], place(half, i), tile_sems.at[half, i]).wait()
+    for i in range(rank // T):
+        for j in range(i):
+            tile = gram_left[i * T : (i + 1) * T, j * T : (j + 1) * T]
+            gram_left[j * T : (j + 1) * T, i * T : (i + 1) * T] = tile.T
+    s = split(sketch[...])
+    cross = split(dot_split(split(gram_left[...]), s))
+    gram = dot_split(s, cross, ((0,), (0,)))
+    for copy in copies:
         copy.wait()
-        x = held[...]
-        out_ref[...] = (dot(x, high, precision=None) + dot(x, low, precision=None)).astype(BF16)
+    tall = [
+        split(dot(held[...], high, precision=None) + dot(held[...], low, precision=None))
+        for held, (high, low) in ((left, s), (right, cross))
+    ]
+    m = split(inverse_factor(gram))
+    left_new_ref[...] = (dot_split(tall[0], m, ((1,), (1,))) * norm).astype(BF16)
+    right_new_ref[...] = (dot_split(tall[1], m, ((1,), (1,))) * (1.0 / norm)).astype(BF16)
 
 
 def truncated(norm, core, mine, theirs, left_core, right_core, target):
     rows, rank = left_core.shape
-    import functools
     out = jax.ShapeDtypeStruct((rows, target), BF16)
     return pl.pallas_call(
         functools.partial(truncate, norm),
         out_shape=(out, out),
-        in_specs=[SMEM, VMEM, VMEM, ANY, ANY],
+        in_specs=[SMEM, ANY, ANY, ANY, ANY],
         out_specs=[VMEM, VMEM],
         scratch_shapes=[
             pltpu.VMEM(left_core.shape, BF16),
             pltpu.VMEM(right_core.shape, BF16),
-            pltpu.VMEM((2, *mine.shape), F32),
             pltpu.VMEM((rank, target), F32),
             pltpu.VMEM((rank, rank), F32),
+            pltpu.SemaphoreType.DMA((2, mine.shape[0])),
             pltpu.SemaphoreType.DMA((2,)),
         ],
+        compiler_params=pltpu.CompilerParams(vmem_limit_bytes=40 << 20),
         name="truncate",
     )(core, mine, theirs, left_core, right_core)
 

time: 104 us -> 95.1 us (0.914)
  Pallas kernels: 21.9 us -> 14.6 us
  other arithmetic: 1.27 us -> 0.2 us
    pallas_call x1, Pallas kernels: 17.6 us -> 11.3 us  [truncated(): pl.pallas_call(functools.partial(truncate, norm), out_shape=(out, out), i...]
    add x1, other arithmetic: 1.13 us -> 0.06 us  [local(): x = keep + lax.ppermute(send, 'grp', swap)]
where the time goes in v2:
time: 95.1 us; the launch traced here: 94.8 us
  blocking collectives  59.9 us (63%)
  starting transfers between devices  16.1 us (17%)
  Pallas kernels  14.6 us (15%)
  waiting for transfers between devices  3.22 us (3%)
    all_to_all x2, blocking collectives, to_all(): lax.all_to_all(jnp.broadcast_to(x, (count, *x.shape)), axes, 0, 0, tiled=...  34.9 us
    all_to_all x1, blocking collectives, local(): lax.all_to_all(x.reshape(plane, -1, 4, T), PLANE, 0, 0, tiled=True).sum(0)  25 us
    pallas_call x1, Pallas kernels, truncated(): pl.pallas_call(functools.partial(truncate, norm), out_shape=(out, out), i...  11.3 us
    ppermute x1, starting transfers between devices, local(): x = keep + lax.ppermute(send, 'grp', swap)  8.75 us
    ppermute x1, starting transfers between devices, local(): theirs = lax.ppermute(mine, 'grp', swap)  7.38 us
    pallas_call x1, Pallas kernels, products(): pl.pallas_call(local_products, out_shape=(half, half), in_specs=[SMEM, AN...  3.23 us
  transfers between devices with their start and end apart: 2, of which 2 were waited for; matrix products, arithmetic and copies ran while one was open for 0% of the time, Pallas kernels for 0%

profile of v2, /device:TPU:1, one launch (start us, length us, event | category | flops | bytes accessed | tf_op | source)
XLA Modules:
  0.0 94.8 jit_solution(7888141550872822672)
XLA Ops:
  0.6 3.2 %products.1 = (f32[9,128,128]{2,1,0:T(8,128)S(1)}, f32[9,128,128]{2,1,0:T(8,128)S(1)}) custom-call(s32[1]{0:T(128)} %bitcast.core_ref, bf16[1024,512]{1,0:T(8,128)(2,1)} %left_hbm.3, bf16[1024,512]{1,0:T(8,128)(2,1)} %right_hbm.3, bf16[1024,256]{1,0:T(8,128)(2,1)} %gauss_hbm.1), custom_call_target="tpu_custom_call" | custom-call | tf_op jit(solution)/shard_map/products/pallas_call | solution.py:76
  3.9 8.7 %collective-permute-start = (f32[9,128,128]{2,1,0:T(8,128)S(1)}, f32[9,128,128]{2,1,0:T(8,128)S(1)}, u32[]{:S(2)}, u32[]{:S(2)}) collective-permute-start(f32[9,128,128]{2,1,0:T(8,128)S(1)} %get-tuple-element.5), channel_id=1, source_target_pairs={{0,1},{1,0},{2,3},{3,2},{4,5},{5,4},{6,7},{7,6},{8,9},{9,8},{10,11... | collective-permute-start | bytes 1769480 | tf_op jit(solution)/shard_map/ppermute | solution.py:261
  12.6 1.6 %collective-permute-done = f32[9,128,128]{2,1,0:T(8,128)S(1)} collective-permute-done((f32[9,128,128]{2,1,0:T(8,128)S(1)}, f32[9,128,128]{2,1,0:T(8,128)S(1)}, u32[]{:S(2)}, u32[]{:S(2)}) %collective-permute-start) | collective-permute-done | bytes 589856 | tf_op jit(solution)/shard_map/ppermute | solution.py:261
  14.2 0.1 add.3
  14.3 25.0 %all_to_all.15 = f32[32,9,4,128]{3,2,1,0:T(4,128)S(1)} all-to-all(f32[32,9,4,128]{3,2,1,0:T(4,128)S(1)} %bitcast.5), channel_id=1, replica_groups=mesh['modes_0'=8,'modes_1'=8,'modes_2'=4,'grp'=2] {'modes_1','modes_2'}, dimensions={0} | all-to-all | bytes 1179648 | tf_op jit(solution)/shard_map/all_to_all | solution.py:262
  39.3 0.1 reduce_sum.18
  39.4 0.0 copy-start.1
  39.4 15.0 %all_to_all.16 = f32[8,9,4,128]{3,2,1,0:T(4,128)S(1)} all-to-all(f32[8,9,4,128]{3,2,1,0:T(4,128)S(1)} %broadcast_in_dim.6), channel_id=1, replica_groups=mesh['modes_0'=8,'modes_1'=8,'modes_2'=4,'grp'=2] {'modes_0'}, dimensions={0} | all-to-all | bytes 294912 | tf_op jit(solution)/shard_map/all_to_all | solution.py:251
  54.4 0.0 copy-start
  54.4 0.1 broadcast_in_dim.7
  54.5 19.9 %all_to_all.17 = f32[32,9,4,128]{3,2,1,0:T(4,128)S(1)} all-to-all(f32[32,9,4,128]{3,2,1,0:T(4,128)S(1)} %broadcast_in_dim.7), channel_id=1, replica_groups=mesh['modes_0'=8,'modes_1'=8,'modes_2'=4,'grp'=2] {'modes_1','modes_2'}, dimensions={0} | all-to-all | bytes 1179648 | tf_op jit(solution)/shard_map/all_to_all | solution.py:251
  74.4 7.4 %collective-permute-start.1 = (f32[9,128,128]{2,1,0:T(8,128)S(1)}, f32[9,128,128]{2,1,0:T(8,128)S(1)}, u32[]{:S(2)}, u32[]{:S(2)}) collective-permute-start(f32[9,128,128]{2,1,0:T(8,128)S(1)} %bitcast.3), channel_id=1, source_target_pairs={{0,1},{1,0},{2,3},{3,2},{4,5},{5,4},{6,7},{7,6},{8,9},{9,8},{10,11... | collective-permute-start | bytes 1769480 | tf_op jit(solution)/shard_map/ppermute | solution.py:265
  81.8 1.6 %collective-permute-done.1.theirs_ref = f32[9,128,128]{2,1,0:T(8,128)S(1)} collective-permute-done((f32[9,128,128]{2,1,0:T(8,128)S(1)}, f32[9,128,128]{2,1,0:T(8,128)S(1)}, u32[]{:S(2)}, u32[]{:S(2)}) %collective-permute-start.1) | collective-permute-done | bytes 589856 | tf_op jit(solution)/shard_map/ppermute | solution.py:265
  83.4 0.0 copy-done.1
  83.4 0.0 copy-done
  83.4 11.3 %truncate.1 = (bf16[1024,256]{1,0:T(8,128)(2,1)}, bf16[1024,256]{1,0:T(8,128)(2,1)}) custom-call(s32[1]{0:T(128)} %bitcast.core_ref, f32[9,128,128]{2,1,0:T(8,128)S(1)} %bitcast.4, f32[9,128,128]{2,1,0:T(8,128)S(1)} %collective-permute-done.1.theirs_ref, bf16[1024,512]{1,0:T(8,128)(2,1)S(1)} %copy-done, bf16[1024,512]{1,0:T(8,128)(2,1)S(1)} %copy-done.1), custom_call_target="tpu_custom_call" | custom-call | tf_op jit(solution)/shard_map/truncate/pallas_call | solution.py:232
  (2 shorter events, 0.1 us)
Async XLA Ops:
  3.9 10.4 %collective-permute-start = (f32[9,128,128]{2,1,0:T(8,128)S(1)}, f32[9,128,128]{2,1,0:T(8,128)S(1)}, u32[]{:S(2)}, u32[]{:S(2)}) collective-permute-start(f32[9,128,128]{2,1,0:T(8,128)S(1)} %get-tuple-element.5), channel_id=1, source_target_pairs={{0,1},{1,0},{2,3},{3,2},{4,5},{5,4},{6,7},{7,6},{8,9},{9,8},{10,11... | collective-permute-start | bytes 1769480 | tf_op jit(solution)/shard_map/ppermute | solution.py:261
  39.4 44.0 %copy-start.1 = (bf16[1024,512]{1,0:T(8,128)(2,1)S(1)}, bf16[1024,512]{1,0:T(8,128)(2,1)}, u32[]{:S(2)}) copy-start(bf16[1024,512]{1,0:T(8,128)(2,1)} %right_hbm.3) | copy-start | bytes 3145732
  54.4 29.0 %copy-start = (bf16[1024,512]{1,0:T(8,128)(2,1)S(1)}, bf16[1024,512]{1,0:T(8,128)(2,1)}, u32[]{:S(2)}) copy-start(bf16[1024,512]{1,0:T(8,128)(2,1)} %left_hbm.3) | copy-start | bytes 3145732
  74.4 9.0 %collective-permute-start.1 = (f32[9,128,128]{2,1,0:T(8,128)S(1)}, f32[9,128,128]{2,1,0:T(8,128)S(1)}, u32[]{:S(2)}, u32[]{:S(2)}) collective-permute-start(f32[9,128,128]{2,1,0:T(8,128)S(1)} %bitcast.3), channel_id=1, source_target_pairs={{0,1},{1,0},{2,3},{3,2},{4,5},{5,4},{6,7},{7,6},{8,9},{9,8},{10,11... | collective-permute-start | bytes 1769480 | tf_op jit(solution)/shard_map/ppermute | solution.py:265

commit v3 on v2

--- a/solution.py
+++ b/solution.py
@@ -9,8 +9,8 @@
 from jax.sharding import Mesh
 from jax.sharding import PartitionSpec as P
 
-GRID = ("modes_0", "modes_1", "modes_2", "grp")
-PLANE = ("modes_1", "modes_2")
+AXIS = "device"
+CHIPS = (8, 8, 4)
 HI = lax.Precision.HIGHEST
 F32, BF16 = jnp.float32, jnp.bfloat16
 T = 128
@@ -247,28 +247,43 @@
     )(core, mine, theirs, left_core, right_core)
 
 
-def to_all(x, axes, count):
-    return lax.all_to_all(jnp.broadcast_to(x, (count, *x.shape)), axes, 0, 0, tiled=True)
+def to_all(x, groups):
+    copies = jnp.broadcast_to(x, (len(groups[0]), *x.shape))
+    return lax.all_to_all(copies, AXIS, 0, 0, axis_index_groups=groups, tiled=True)
+
+
+def groups_of(grid):
+    first, second, third = grid
+
+    def device(i, j, k, core):
+        return ((i * second + j) * third + k) * 2 + core
+
+    scatter = [[device(i, j, k, 0) for j in range(second) for k in range(third)] for i in range(first)]
+    scatter += [[device(i, j, k, 1) for i in range(first) for k in range(third)] for j in range(second)]
+    exchange = [[device(i, j, k, 0) for i in range(first)] for j in range(second) for k in range(third)]
+    exchange += [[device(i, j, k, 1) for j in range(second)] for i in range(first) for k in range(third)]
+    return scatter, exchange
 
 
 def local(left_core, right_core, gauss_core):
-    devices = math.prod(lax.axis_size(a) for a in GRID)
-    plane = lax.axis_size(PLANE[0]) * lax.axis_size(PLANE[1])
+    devices = math.prod(CHIPS) * 2
     norm = math.sqrt(left_core.shape[0] * devices)
-    core = lax.axis_index("grp").reshape(1)
-    swap = [(0, 1), (1, 0)]
+    core = (lax.axis_index(AXIS) % 2).reshape(1)
+    swap = [(i, i ^ 1) for i in range(devices)]
+    scatter, exchange = groups_of(CHIPS)
     keep, send = products(core, left_core, right_core, gauss_core)
-    x = keep + lax.ppermute(send, "grp", swap)
-    x = lax.all_to_all(x.reshape(plane, -1, 4, T), PLANE, 0, 0, tiled=True).sum(0)
-    x = to_all(x, "modes_0", lax.axis_size("modes_0")).reshape(-1, *x.shape).sum(0)
-    mine = to_all(x, PLANE, plane).reshape(keep.shape)
-    theirs = lax.ppermute(mine, "grp", swap)
+    x = keep + lax.ppermute(send, AXIS, swap)
+    x = x.reshape(len(scatter[0]), -1, 4, T)
+    x = lax.all_to_all(x, AXIS, 0, 0, axis_index_groups=scatter, tiled=True).sum(0)
+    x = to_all(x, exchange).reshape(-1, *x.shape).sum(0)
+    mine = to_all(x, scatter).reshape(keep.shape)
+    theirs = lax.ppermute(mine, AXIS, swap)
     return truncated(norm, core, mine, theirs, left_core, right_core, gauss_core.shape[1])
 
 
 def solution(mesh):
-    finer = Mesh(mesh.devices.reshape(8, 8, 4, mesh.shape["grp"]), GRID)
-    spec = P(GRID, None)
+    flat = Mesh(mesh.devices.reshape(-1), (AXIS,))
+    spec = P(AXIS, None)
     return jax.shard_map(
-        local, mesh=finer, in_specs=(spec, spec, spec), out_specs=(spec, spec), check_vma=False
+        local, mesh=flat, in_specs=(spec, spec, spec), out_specs=(spec, spec), check_vma=False
     )

time: 95.1 us -> 87.2 us (0.917)
  blocking collectives: 59.9 us -> 53.4 us
  starting transfers between devices: 16.1 us -> 14.7 us
    all_to_all x3, blocking collectives: 59.9 us -> 53.4 us  [the longest x2 36 us: to_all(): lax.all_to_all(copies, AXIS, 0, 0, axis_index_groups=groups, tiled=True)]
    ppermute x2, starting transfers between devices: 16.1 us -> 14.7 us  [the longest x1 8.75 us: local(): x = keep + lax.ppermute(send, AXIS, swap)]
where the time goes in v3:
time: 87.2 us; the launch traced here: 86.9 us
  blocking collectives  53.4 us (61%)
  starting transfers between devices  14.7 us (17%)
  Pallas kernels  14.5 us (17%)
  waiting for transfers between devices  3.22 us (4%)
    all_to_all x2, blocking collectives, to_all(): lax.all_to_all(copies, AXIS, 0, 0, axis_index_groups=groups, tiled=True)  36 us
    all_to_all x1, blocking collectives, local(): lax.all_to_all(x, AXIS, 0, 0, axis_index_groups=scatter, tiled=True).sum(0)  17.4 us
    pallas_call x1, Pallas kernels, truncated(): pl.pallas_call(functools.partial(truncate, norm), out_shape=(out, out), i...  11.3 us
    ppermute x1, starting transfers between devices, local(): x = keep + lax.ppermute(send, AXIS, swap)  8.75 us
    ppermute x1, starting transfers between devices, local(): theirs = lax.ppermute(mine, AXIS, swap)  5.98 us
    pallas_call x1, Pallas kernels, products(): pl.pallas_call(local_products, out_shape=(half, half), in_specs=[SMEM, AN...  3.23 us
  transfers between devices with their start and end apart: 2, of which 2 were waited for; matrix products, arithmetic and copies ran while one was open for 0% of the time, Pallas kernels for 0%

profile of v3, /device:TPU:1, one launch (start us, length us, event | category | flops | bytes accessed | tf_op | source)
XLA Modules:
  0.0 86.9 jit_solution(1976206324416186999)
XLA Ops:
  0.6 3.2 %products.1 = (f32[9,128,128]{2,1,0:T(8,128)S(1)}, f32[9,128,128]{2,1,0:T(8,128)S(1)}) custom-call(s32[1]{0:T(128)} %bitcast.core_ref, bf16[1024,512]{1,0:T(8,128)(2,1)} %left_hbm.3, bf16[1024,512]{1,0:T(8,128)(2,1)} %right_hbm.3, bf16[1024,256]{1,0:T(8,128)(2,1)} %gauss_hbm.1), custom_call_target="tpu_custom_call" | custom-call | tf_op jit(solution)/shard_map/products/pallas_call | solution.py:76
  3.9 8.7 %collective-permute-start = (f32[9,128,128]{2,1,0:T(8,128)S(1)}, f32[9,128,128]{2,1,0:T(8,128)S(1)}, u32[]{:S(2)}, u32[]{:S(2)}) collective-permute-start(f32[9,128,128]{2,1,0:T(8,128)S(1)} %get-tuple-element.5), channel_id=1, source_target_pairs={{0,1},{1,0},{2,3},{3,2},{4,5},{5,4},{6,7},{7,6},{8,9},{9,8},{10,11... | collective-permute-start | bytes 1769480 | tf_op jit(solution)/shard_map/ppermute | solution.py:275
  12.6 1.6 %collective-permute-done = f32[9,128,128]{2,1,0:T(8,128)S(1)} collective-permute-done((f32[9,128,128]{2,1,0:T(8,128)S(1)}, f32[9,128,128]{2,1,0:T(8,128)S(1)}, u32[]{:S(2)}, u32[]{:S(2)}) %collective-permute-start) | collective-permute-done | bytes 589856 | tf_op jit(solution)/shard_map/ppermute | solution.py:275
  14.2 0.1 add.8
  14.3 17.4 %all_to_all.15 = f32[32,9,4,128]{3,2,1,0:T(4,128)S(1)} all-to-all(f32[32,9,4,128]{3,2,1,0:T(4,128)S(1)} %bitcast.5), channel_id=1, replica_groups={{0,2,4,6,8,10,12,14,16,18,20,22,24,26,28,30,32,34,36,38,40,42,44,46,48,..., dimensions={0} | all-to-all | bytes 1179648 | tf_op jit(solution)/shard_map/all_to_all | solution.py:277
  31.7 0.1 reduce_sum.18
  31.8 0.0 copy-start.1
  31.8 18.0 %all_to_all.16 = f32[8,9,4,128]{3,2,1,0:T(4,128)S(1)} all-to-all(f32[8,9,4,128]{3,2,1,0:T(4,128)S(1)} %broadcast_in_dim.6), channel_id=1, replica_groups={{0,64,128,192,256,320,384,448},{2,66,130,194,258,322,386,450},{4,68,132..., dimensions={0} | all-to-all | bytes 294912 | tf_op jit(solution)/shard_map/all_to_all | solution.py:252
  49.9 0.0 copy-start
  49.9 0.1 broadcast_in_dim.7
  50.0 18.0 %all_to_all.17 = f32[32,9,4,128]{3,2,1,0:T(4,128)S(1)} all-to-all(f32[32,9,4,128]{3,2,1,0:T(4,128)S(1)} %broadcast_in_dim.7), channel_id=1, replica_groups={{0,2,4,6,8,10,12,14,16,18,20,22,24,26,28,30,32,34,36,38,40,42,44,46,48,..., dimensions={0} | all-to-all | bytes 1179648 | tf_op jit(solution)/shard_map/all_to_all | solution.py:252
  68.0 6.0 %collective-permute-start.1 = (f32[9,128,128]{2,1,0:T(8,128)S(1)}, f32[9,128,128]{2,1,0:T(8,128)S(1)}, u32[]{:S(2)}, u32[]{:S(2)}) collective-permute-start(f32[9,128,128]{2,1,0:T(8,128)S(1)} %bitcast.3), channel_id=1, source_target_pairs={{0,1},{1,0},{2,3},{3,2},{4,5},{5,4},{6,7},{7,6},{8,9},{9,8},{10,11... | collective-permute-start | bytes 1769480 | tf_op jit(solution)/shard_map/ppermute | solution.py:280
  74.0 1.6 %collective-permute-done.1.theirs_ref = f32[9,128,128]{2,1,0:T(8,128)S(1)} collective-permute-done((f32[9,128,128]{2,1,0:T(8,128)S(1)}, f32[9,128,128]{2,1,0:T(8,128)S(1)}, u32[]{:S(2)}, u32[]{:S(2)}) %collective-permute-start.1) | collective-permute-done | bytes 589856 | tf_op jit(solution)/shard_map/ppermute | solution.py:280
  75.6 0.0 copy-done.1
  75.6 0.0 copy-done
  75.6 11.3 %truncate.1 = (bf16[1024,256]{1,0:T(8,128)(2,1)}, bf16[1024,256]{1,0:T(8,128)(2,1)}) custom-call(s32[1]{0:T(128)} %bitcast.core_ref, f32[9,128,128]{2,1,0:T(8,128)S(1)} %bitcast.4, f32[9,128,128]{2,1,0:T(8,128)S(1)} %collective-permute-done.1.theirs_ref, bf16[1024,512]{1,0:T(8,128)(2,1)S(1)} %copy-done, bf16[1024,512]{1,0:T(8,128)(2,1)S(1)} %copy-done.1), custom_call_target="tpu_custom_call" | custom-call | tf_op jit(solution)/shard_map/truncate/pallas_call | solution.py:232
  (2 shorter events, 0.1 us)
Async XLA Ops:
  3.9 10.4 %collective-permute-start = (f32[9,128,128]{2,1,0:T(8,128)S(1)}, f32[9,128,128]{2,1,0:T(8,128)S(1)}, u32[]{:S(2)}, u32[]{:S(2)}) collective-permute-start(f32[9,128,128]{2,1,0:T(8,128)S(1)} %get-tuple-element.5), channel_id=1, source_target_pairs={{0,1},{1,0},{2,3},{3,2},{4,5},{5,4},{6,7},{7,6},{8,9},{9,8},{10,11... | collective-permute-start | bytes 1769480 | tf_op jit(solution)/shard_map/ppermute | solution.py:275
  31.8 43.7 %copy-start.1 = (bf16[1024,512]{1,0:T(8,128)(2,1)S(1)}, bf16[1024,512]{1,0:T(8,128)(2,1)}, u32[]{:S(2)}) copy-start(bf16[1024,512]{1,0:T(8,128)(2,1)} %right_hbm.3) | copy-start | bytes 3145732
  49.9 25.7 %copy-start = (bf16[1024,512]{1,0:T(8,128)(2,1)S(1)}, bf16[1024,512]{1,0:T(8,128)(2,1)}, u32[]{:S(2)}) copy-start(bf16[1024,512]{1,0:T(8,128)(2,1)} %left_hbm.3) | copy-start | bytes 3145732
  68.0 7.6 %collective-permute-start.1 = (f32[9,128,128]{2,1,0:T(8,128)S(1)}, f32[9,128,128]{2,1,0:T(8,128)S(1)}, u32[]{:S(2)}, u32[]{:S(2)}) collective-permute-start(f32[9,128,128]{2,1,0:T(8,128)S(1)} %bitcast.3), channel_id=1, source_target_pairs={{0,1},{1,0},{2,3},{3,2},{4,5},{5,4},{6,7},{7,6},{8,9},{9,8},{10,11... | collective-permute-start | bytes 1769480 | tf_op jit(solution)/shard_map/ppermute | solution.py:280

commit v4 on v3

--- a/solution.py
+++ b/solution.py
@@ -16,6 +16,8 @@
 T = 128
 SUB = 8
 OUTER = 32
+BESIDE = (1, 4)
+TAIL = 1
 ANY = pl.BlockSpec(memory_space=pl.ANY)
 VMEM = pl.BlockSpec(memory_space=pltpu.VMEM)
 SMEM = pl.BlockSpec(memory_space=pltpu.SMEM)
@@ -32,59 +34,62 @@
     return both[: len(both) // 2], both[len(both) // 2 :]
 
 
-def local_products(core_ref, left_hbm, right_hbm, gauss_hbm, keep_ref, send_ref, left, right, gauss, sems):
-    copies = [
-        pltpu.make_async_copy(src, dst, sems.at[i])
-        for i, (src, dst) in enumerate(((right_hbm, right), (gauss_hbm, gauss), (left_hbm, left)))
-    ]
-    for copy in copies:
-        copy.start()
+def local_products(given, core_ref, left_hbm, right_hbm, gauss_hbm, out_ref, left, right, gauss, sems):
     rank, target = right.shape[1], gauss.shape[1]
     halves = tiles_of(rank, target)
-    core = core_ref[0]
-
-    def put(kind, col, value, first):
+
+    def put(half, kind, col, value, first):
         for i in range(value.shape[0] // T):
-            tile = (kind, first + i, col)
-            half = 0 if tile in halves[0] else 1
-            place = halves[half].index(tile)
-            block = value[i * T : (i + 1) * T, :]
-
-            @pl.when(core == half)
-            def _():
-                keep_ref[place] = block
-
-            @pl.when(core != half)
-            def _():
-                send_ref[place] = block
-
-    copies[0].wait()
-    copies[1].wait()
-    x = dot(right[...], gauss[...], ((0,), (0,)), None)
-    for j in range(target // T):
-        put("s", j, x[:, j * T : (j + 1) * T], 0)
-    copies[2].wait()
-    for j in range(0, rank // T, 2):
-        y = dot(left[:, j * T :], left[:, j * T : (j + 2) * T], ((0,), (0,)), None)
-        put("g", j, y[:, :T], j)
-        put("g", j + 1, y[T:, T:], j + 1)
-
-
-def products(core, left_core, right_core, gauss_core):
-    rank, target = right_core.shape[1], gauss_core.shape[1]
-    half = pltpu.VMEM((len(tiles_of(rank, target)[0]), T, T), F32)
+            if (kind, first + i, col) in halves[half]:
+                out_ref[halves[half].index((kind, first + i, col))] = value[i * T : (i + 1) * T, :]
+
+    def sketch_half():
+        corner = left.at[:, pl.ds(0, T)]
+        copies = [
+            pltpu.make_async_copy(right_hbm, right, sems.at[0]),
+            pltpu.make_async_copy(gauss_hbm, gauss, sems.at[1]),
+            pltpu.make_async_copy(left_hbm.at[:, pl.ds(0, T)], corner, sems.at[2]),
+        ]
+        for copy in copies:
+            copy.start()
+        for copy in copies:
+            copy.wait()
+        x = dot(right[...], gauss[...], ((0,), (0,)), None)
+        for j in range(target // T):
+            put(0, "s", j, x[:, j * T : (j + 1) * T], 0)
+        put(0, "g", 0, dot(corner[...], corner[...], ((0,), (0,)), None), 0)
+
+    def gram_half():
+        copy = pltpu.make_async_copy(left_hbm, left, sems.at[0])
+        copy.start()
+        copy.wait()
+        for j in range(0, rank // T, 2):
+            y = dot(left[:, j * T :], left[:, j * T : (j + 2) * T], ((0,), (0,)), None)
+            put(1, "g", j, y[:, :T], j)
+            put(1, "g", j + 1, y[T:, T:], j + 1)
+
+    pl.when(core_ref[0] == given)(sketch_half)
+    pl.when(core_ref[0] != given)(gram_half)
+
+
+def products(given, core, left_core, right_core, gauss_core):
+    rows, rank = left_core.shape
+    target = gauss_core.shape[1]
     return pl.pallas_call(
-        local_products,
-        out_shape=(half, half),
+        functools.partial(local_products, given),
+        out_shape=pltpu.VMEM((len(tiles_of(rank, target)[0]), T, T), F32),
         in_specs=[SMEM, ANY, ANY, ANY],
-        out_specs=[VMEM, VMEM],
+        out_specs=VMEM,
         scratch_shapes=[
             pltpu.VMEM(left_core.shape, BF16),
             pltpu.VMEM(right_core.shape, BF16),
             pltpu.VMEM(gauss_core.shape, BF16),
             pltpu.SemaphoreType.DMA((3,)),
         ],
-        name="products",
+        cost_estimate=pl.CostEstimate(
+            flops=2 * rows * rank * target, bytes_accessed=3 * rows * rank, transcendentals=0
+        ),
+        name=f"products_{given}",
     )(core, left_core, right_core, gauss_core)
 
 
@@ -114,13 +119,14 @@
     return dot(xh, yh, dims, None) + (dot(xh, yl, dims, None) + dot(xl, yh, dims, None))
 
 
-def inverse_factor(a):
+def inverse_factor(a, beside):
     n = a.shape[0]
     parts = range(n // T)
     sub = lax.broadcasted_iota(jnp.int32, (SUB, T), 0)
     lanes = [lax.broadcasted_iota(jnp.int32, (SUB, T), 1) + T * h for h in parts]
     done = []
     for first in range(0, n, OUTER):
+        beside(first // OUTER)
         block = a[first : first + OUTER, :]
         if first:
             u = jnp.concatenate(done, 0)
@@ -179,8 +185,9 @@
     return jnp.where(row >= col, m, 0.0)
 
 
-def truncate(norm, core_ref, mine_ref, theirs_ref, left_hbm, right_hbm, left_new_ref, right_new_ref,
-             left, right, sketch, gram_left, tile_sems, sems):
+def truncate(norm, core_ref, mine_ref, theirs_ref, left_hbm, right_hbm, left_new_hbm, right_new_hbm,
+             left, right, sketch, gram_left, left_out, right_out,
+             tile_sems, sems, out_sems):
     rank, target = sketch.shape
     halves = tiles_of(rank, target)
     core = core_ref[0]
@@ -217,13 +224,31 @@
     gram = dot_split(s, cross, ((0,), (0,)))
     for copy in copies:
         copy.wait()
-    tall = [
-        split(dot(held[...], high, precision=None) + dot(held[...], low, precision=None))
-        for held, (high, low) in ((left, s), (right, cross))
-    ]
-    m = split(inverse_factor(gram))
-    left_new_ref[...] = (dot_split(tall[0], m, ((1,), (1,))) * norm).astype(BF16)
-    right_new_ref[...] = (dot_split(tall[1], m, ((1,), (1,))) * (1.0 / norm)).astype(BF16)
+    tall = []
+
+    def beside(step):
+        for held, (high, low), when in ((left, s, BESIDE[0]), (right, cross, BESIDE[1])):
+            if step == when:
+                x = held[...]
+                tall.append(split(dot(x, high, precision=None) + dot(x, low, precision=None)))
+
+    m = split(inverse_factor(gram, beside))
+    chunk_out = left.shape[0] // TAIL
+    outs = []
+    for scale, (heads, rests), staged, out_hbm in (
+        (norm, tall[0], left_out, left_new_hbm),
+        (1.0 / norm, tall[1], right_out, right_new_hbm),
+    ):
+        for part in range(TAIL):
+            at = pl.ds(part * chunk_out, chunk_out)
+            rows = slice(part * chunk_out, (part + 1) * chunk_out)
+            x = dot_split((heads[rows, :], rests[rows, :]), m, ((1,), (1,)))
+            staged[at, :] = (x * scale).astype(BF16)
+            out = pltpu.make_async_copy(staged.at[at, :], out_hbm.at[at, :], out_sems.at[len(outs)])
+            out.start()
+            outs.append(out)
+    for out in outs:
+        out.wait()
 
 
 def truncated(norm, core, mine, theirs, left_core, right_core, target):
@@ -233,14 +258,16 @@
         functools.partial(truncate, norm),
         out_shape=(out, out),
         in_specs=[SMEM, ANY, ANY, ANY, ANY],
-        out_specs=[VMEM, VMEM],
+        out_specs=[ANY, ANY],
         scratch_shapes=[
             pltpu.VMEM(left_core.shape, BF16),
             pltpu.VMEM(right_core.shape, BF16),
             pltpu.VMEM((rank, target), F32),
             pltpu.VMEM((rank, rank), F32),
+            *[pltpu.VMEM((rows, target), BF16)] * 2,
             pltpu.SemaphoreType.DMA((2, mine.shape[0])),
             pltpu.SemaphoreType.DMA((2,)),
+            pltpu.SemaphoreType.DMA((2 * TAIL,)),
         ],
         compiler_params=pltpu.CompilerParams(vmem_limit_bytes=40 << 20),
         name="truncate",
@@ -271,8 +298,9 @@
     core = (lax.axis_index(AXIS) % 2).reshape(1)
     swap = [(i, i ^ 1) for i in range(devices)]
     scatter, exchange = groups_of(CHIPS)
-    keep, send = products(core, left_core, right_core, gauss_core)
-    x = keep + lax.ppermute(send, AXIS, swap)
+    theirs = lax.ppermute(products(1, core, left_core, right_core, gauss_core), AXIS, swap)
+    keep = products(0, core, left_core, right_core, gauss_core)
+    x = keep + theirs
     x = x.reshape(len(scatter[0]), -1, 4, T)
     x = lax.all_to_all(x, AXIS, 0, 0, axis_index_groups=scatter, tiled=True).sum(0)
     x = to_all(x, exchange).reshape(-1, *x.shape).sum(0)

time: 87.2 us -> 85.5 us (0.981)
  waiting for transfers between devices: 3.22 us -> 1.61 us
    ppermute x1, waiting for transfers between devices: 1.61 us -> 0.01 us  [local(): lax.ppermute(products(1, core, left_core, right_core, gauss_core), AXIS,...]
    pallas_call x1 -> x2, Pallas kernels: 3.23 us -> 3.88 us  [products(): pl.pallas_call(functools.partial(local_products, given), out_shape=pltpu....]
  transfers between devices with their start and end apart: 2 -> 2, of which waited for: 2 -> 1; matrix products, arithmetic and copies ran while one was open for 0% -> 0% of each run, Pallas kernels for 0% -> 2%
where the time goes in v4:
time: 85.5 us; the launch traced here: 85.2 us
  blocking collectives  53.5 us (63%)
  Pallas kernels  14.8 us (17%)
  starting transfers between devices  14.2 us (17%)
  waiting for transfers between devices  1.61 us (2%)
    all_to_all x2, blocking collectives, to_all(): lax.all_to_all(copies, AXIS, 0, 0, axis_index_groups=groups, tiled=True)  35.9 us
    all_to_all x1, blocking collectives, local(): lax.all_to_all(x, AXIS, 0, 0, axis_index_groups=scatter, tiled=True).sum(0)  17.6 us
    pallas_call x1, Pallas kernels, truncated(): pl.pallas_call(functools.partial(truncate, norm), out_shape=(out, out), i...  10.9 us
    ppermute x1, starting transfers between devices, local(): lax.ppermute(products(1, core, left_core, right_core, gauss_core), AXIS,...  8.63 us
    ppermute x1, starting transfers between devices, local(): theirs = lax.ppermute(mine, AXIS, swap)  5.61 us
    pallas_call x2, Pallas kernels, products(): pl.pallas_call(functools.partial(local_products, given), out_shape=pltpu....  3.88 us
  transfers between devices with their start and end apart: 2, of which 1 were waited for; matrix products, arithmetic and copies ran while one was open for 0% of the time, Pallas kernels for 2%

profile of v4, /device:TPU:1, one launch (start us, length us, event | category | flops | bytes accessed | tf_op | source)
XLA Modules:
  0.0 85.2 jit_solution(10600757717055140512)
XLA Ops:
  0.6 2.0 %products_1.1 = f32[9,128,128]{2,1,0:T(8,128)S(1)} custom-call(s32[1]{0:T(128)} %bitcast.core_ref, bf16[1024,512]{1,0:T(8,128)(2,1)} %left_hbm.5, bf16[1024,512]{1,0:T(8,128)(2,1)} %right_hbm.5, bf16[1024,256]{1,0:T(8,128)(2,1)} %gauss_hbm.3), custom_call_target="tpu_custom_call" | custom-call | flops 268435456 | bytes 1572864 | tf_op jit(solution)/shard_map/products_1/pallas_call | solution.py:78
  2.6 8.6 %collective-permute-start = (f32[9,128,128]{2,1,0:T(8,128)S(1)}, f32[9,128,128]{2,1,0:T(8,128)S(1)}, u32[]{:S(2)}, u32[]{:S(2)}) collective-permute-start(f32[9,128,128]{2,1,0:T(8,128)S(1)} %products_1.1), channel_id=1, source_target_pairs={{0,1},{1,0},{2,3},{3,2},{4,5},{5,4},{6,7},{7,6},{8,9},{9,8},{10,11... | collective-permute-start | bytes 1769480 | tf_op jit(solution)/shard_map/ppermute | solution.py:301
  11.3 1.9 %products_0.1 = f32[9,128,128]{2,1,0:T(8,128)S(1)} custom-call(s32[1]{0:T(128)} %bitcast.core_ref, bf16[1024,512]{1,0:T(8,128)(2,1)} %left_hbm.5, bf16[1024,512]{1,0:T(8,128)(2,1)} %right_hbm.5, bf16[1024,256]{1,0:T(8,128)(2,1)} %gauss_hbm.3), custom_call_target="tpu_custom_call" | custom-call | flops 268435456 | bytes 1572864 | tf_op jit(solution)/shard_map/products_0/pallas_call | solution.py:78
  13.2 0.0 collective-permute-done
  13.2 0.1 add.8
  13.2 17.6 %all_to_all.15 = f32[32,9,4,128]{3,2,1,0:T(4,128)S(1)} all-to-all(f32[32,9,4,128]{3,2,1,0:T(4,128)S(1)} %bitcast.5), channel_id=1, replica_groups={{0,2,4,6,8,10,12,14,16,18,20,22,24,26,28,30,32,34,36,38,40,42,44,46,48,..., dimensions={0} | all-to-all | bytes 1179648 | tf_op jit(solution)/shard_map/all_to_all | solution.py:305
  30.9 0.1 reduce_sum.18
  31.0 0.0 copy-start.1
  31.0 17.8 %all_to_all.16 = f32[8,9,4,128]{3,2,1,0:T(4,128)S(1)} all-to-all(f32[8,9,4,128]{3,2,1,0:T(4,128)S(1)} %broadcast_in_dim.6), channel_id=1, replica_groups={{0,64,128,192,256,320,384,448},{2,66,130,194,258,322,386,450},{4,68,132..., dimensions={0} | all-to-all | bytes 294912 | tf_op jit(solution)/shard_map/all_to_all | solution.py:279
  48.8 0.0 copy-start
  48.8 0.1 broadcast_in_dim.7
  48.9 18.1 %all_to_all.17 = f32[32,9,4,128]{3,2,1,0:T(4,128)S(1)} all-to-all(f32[32,9,4,128]{3,2,1,0:T(4,128)S(1)} %broadcast_in_dim.7), channel_id=1, replica_groups={{0,2,4,6,8,10,12,14,16,18,20,22,24,26,28,30,32,34,36,38,40,42,44,46,48,..., dimensions={0} | all-to-all | bytes 1179648 | tf_op jit(solution)/shard_map/all_to_all | solution.py:279
  67.0 5.6 %collective-permute-start.1 = (f32[9,128,128]{2,1,0:T(8,128)S(1)}, f32[9,128,128]{2,1,0:T(8,128)S(1)}, u32[]{:S(2)}, u32[]{:S(2)}) collective-permute-start(f32[9,128,128]{2,1,0:T(8,128)S(1)} %bitcast.3), channel_id=1, source_target_pairs={{0,1},{1,0},{2,3},{3,2},{4,5},{5,4},{6,7},{7,6},{8,9},{9,8},{10,11... | collective-permute-start | bytes 1769480 | tf_op jit(solution)/shard_map/ppermute | solution.py:308
  72.7 1.6 %collective-permute-done.1.theirs_ref = f32[9,128,128]{2,1,0:T(8,128)S(1)} collective-permute-done((f32[9,128,128]{2,1,0:T(8,128)S(1)}, f32[9,128,128]{2,1,0:T(8,128)S(1)}, u32[]{:S(2)}, u32[]{:S(2)}) %collective-permute-start.1) | collective-permute-done | bytes 589856 | tf_op jit(solution)/shard_map/ppermute | solution.py:308
  74.3 0.0 copy-done.1
  74.3 0.0 copy-done
  74.3 10.9 %truncate.1 = (bf16[1024,256]{1,0:T(8,128)(2,1)}, bf16[1024,256]{1,0:T(8,128)(2,1)}) custom-call(s32[1]{0:T(128)} %bitcast.core_ref, f32[9,128,128]{2,1,0:T(8,128)S(1)} %bitcast.4, f32[9,128,128]{2,1,0:T(8,128)S(1)} %collective-permute-done.1.theirs_ref, bf16[1024,512]{1,0:T(8,128)(2,1)S(1)} %copy-done, bf16[1024,512]{1,0:T(8,128)(2,1)S(1)} %copy-done.1), custom_call_target="tpu_custom_call" | custom-call | tf_op jit(solution)/shard_map/truncate/pallas_call | solution.py:257
  (2 shorter events, 0.1 us)
Async XLA Ops:
  2.6 10.5 %collective-permute-start = (f32[9,128,128]{2,1,0:T(8,128)S(1)}, f32[9,128,128]{2,1,0:T(8,128)S(1)}, u32[]{:S(2)}, u32[]{:S(2)}) collective-permute-start(f32[9,128,128]{2,1,0:T(8,128)S(1)} %products_1.1), channel_id=1, source_target_pairs={{0,1},{1,0},{2,3},{3,2},{4,5},{5,4},{6,7},{7,6},{8,9},{9,8},{10,11... | collective-permute-start | bytes 1769480 | tf_op jit(solution)/shard_map/ppermute | solution.py:301
  31.0 43.2 %copy-start.1 = (bf16[1024,512]{1,0:T(8,128)(2,1)S(1)}, bf16[1024,512]{1,0:T(8,128)(2,1)}, u32[]{:S(2)}) copy-start(bf16[1024,512]{1,0:T(8,128)(2,1)} %right_hbm.5) | copy-start | bytes 3145732
  48.8 25.5 %copy-start = (bf16[1024,512]{1,0:T(8,128)(2,1)S(1)}, bf16[1024,512]{1,0:T(8,128)(2,1)}, u32[]{:S(2)}) copy-start(bf16[1024,512]{1,0:T(8,128)(2,1)} %left_hbm.5) | copy-start | bytes 3145732
  67.0 7.2 %collective-permute-start.1 = (f32[9,128,128]{2,1,0:T(8,128)S(1)}, f32[9,128,128]{2,1,0:T(8,128)S(1)}, u32[]{:S(2)}, u32[]{:S(2)}) collective-permute-start(f32[9,128,128]{2,1,0:T(8,128)S(1)} %bitcast.3), channel_id=1, source_target_pairs={{0,1},{1,0},{2,3},{3,2},{4,5},{5,4},{6,7},{7,6},{8,9},{9,8},{10,11... | collective-permute-start | bytes 1769480 | tf_op jit(solution)/shard_map/ppermute | solution.py:308
